TPU v7x, 256 devices: a whole 4x4x8 slice. The times are simulated.
256 devices in a mesh: dp: 8 (over z), bin: 32 (over x, y, core).
Axes of the slice: x: 4, y: 4, z: 8, core: 2. Of those that a mesh axis runs over, the one named last changes fastest.
Arguments:
- embeddings: bfloat16 [196608, 256], P(('dp', 'bin')), may hold values from -8 to 8
- bin_ids: int32 [196608], P(('dp', 'bin')), may hold values from 0 to 31, as said below
- spreads: float32 [3], replicated, may hold values from 0.5 to 4
- projection: bfloat16 [256, 256], replicated, may hold values from -0.375 to 0.375
Outputs:
- grad_emb: bfloat16 [196608, 256], P(('dp', 'bin'))
- grad_w: float32 [256, 256], replicated
- loss: float32 [], replicated
Inputs may be any that keep to these rules, and one draw needn't show every extreme that they name: `bin_ids`: among the 768 jets of one device at most 48 share a mass bin, and on every device one bin holds exactly 48 of them.
All inputs are finite; a program needn't handle non-finite values.
Results may differ from a plain program's by a relative error of at most 0.0044.
The roundings to bfloat16 on the way count: a program that leaves them out, or rounds other values in their place, can miss the bound.
Values may be sent and summed in bfloat16 or wider, within the bound.
A program may use at most 64 MiB of HBM per device.

v0:
```python
import jax
import jax.numpy as jnp
from jax import lax
from jax.sharding import PartitionSpec as P


def from_partner(value, axis, bit):
    mask = 2**bit
    pairs = [(source, source ^ mask) for source in range(lax.axis_size(axis))]
    return lax.ppermute(value, axis, pairs)


def tile_terms(xa, mask_a, xb, mask_b, inv_bw):
    rows_a, width = xa.shape
    rows_b = xb.shape[0]
    block = 512
    count = rows_a // block
    sq_b = jnp.sum(jnp.square(xb.astype(jnp.float32)), 1)
    coef = inv_bw / width

    def step(carry, item):
        total, col_sum, back = carry
        xblk, mblk = item
        inner = lax.dot_general(
            xblk, xb, (((1,), (1,)), ((), ())), preferred_element_type=jnp.float32
        )
        sq_a = jnp.sum(jnp.square(xblk.astype(jnp.float32)), 1)
        dist = sq_a[:, None] + sq_b[None, :] - 2.0 * inner
        kern = jnp.zeros(dist.shape, jnp.float32)
        weight = jnp.zeros(dist.shape, jnp.float32)
        for index in range(coef.shape[0]):
            expo = jnp.exp(-dist * coef[index])
            kern = kern + expo
            weight = weight + coef[index] * expo
        pairs = mblk[:, None] * mask_b[None, :]
        total = total + jnp.sum(kern * pairs)
        gram = (weight * pairs).astype(jnp.bfloat16)
        gram_f = gram.astype(jnp.float32)
        part_a = xblk.astype(jnp.float32) * jnp.sum(gram_f, 1)[:, None] - jnp.dot(
            gram, xb, preferred_element_type=jnp.float32
        )
        return ((total, col_sum, back), part_a)

    init = (
        jnp.zeros((), jnp.float32),
        jnp.zeros((rows_b,), jnp.float32),
        jnp.zeros((rows_b, width), jnp.float32),
    )
    (total, col_sum, back), parts = lax.scan(
        step, init, (xa.reshape(count, block, width), mask_a.reshape(count, block))
    )
    part_a = parts.reshape(rows_a, width)
    part_b = xb.astype(jnp.float32) * col_sum[:, None] - back
    return (total, part_a, part_b)


def local(embeddings, bin_ids, spreads, projection):
    rows, width = embeddings.shape
    owners = lax.axis_size("bin")
    slots_per = 2 * rows // owners
    inv_bw = 1.0 / spreads
    feats = jnp.dot(embeddings, projection, preferred_element_type=jnp.float32).astype(jnp.bfloat16)
    onehot = (bin_ids[:, None] == jnp.arange(owners, dtype=jnp.int32)[None, :]).astype(jnp.int32)
    counts = jnp.sum(onehot, 0)
    slot = jnp.sum((jnp.cumsum(onehot, 0) - 1) * onehot, 1)
    outbox = jnp.zeros((owners, slots_per, width), jnp.bfloat16).at[bin_ids, slot].set(feats)
    inbox, arrived = (
        lax.all_to_all(outbox, "bin", split_axis=0, concat_axis=0, tiled=True),
        lax.all_to_all(counts[:, None], "bin", split_axis=0, concat_axis=0, tiled=True),
    )
    mine = inbox.reshape(owners * slots_per, width)
    slot_ids = jnp.arange(slots_per, dtype=jnp.int32)[None, :]
    live = (slot_ids < arrived).astype(jnp.float32).reshape(-1)
    own_n = jnp.maximum(jnp.sum(arrived).astype(jnp.float32), 1.0)
    bit = owners.bit_length() - 2
    partner, partner_arrived = from_partner((mine, arrived), "bin", bit)
    partner_live = (slot_ids < partner_arrived).astype(jnp.float32).reshape(-1)
    partner_n = jnp.maximum(jnp.sum(partner_arrived).astype(jnp.float32), 1.0)
    self_sum, self_part, unused = tile_terms(mine, live, mine, live, inv_bw)
    cross_sum, cross_part, spare = tile_terms(mine, live, partner, partner_live, inv_bw)
    cross_loss = -cross_sum / (own_n * partner_n)
    scale = float(rows * width)
    grad_feat = (
        scale * (-(4.0 / (own_n * own_n)) * self_part + 4.0 / (own_n * partner_n) * cross_part)
    ).astype(jnp.bfloat16)
    local_loss = self_sum / (own_n * own_n) + cross_loss
    homeward = lax.all_to_all(
        grad_feat.reshape(owners, slots_per, width), "bin", split_axis=0, concat_axis=0, tiled=True
    )
    grad_rows = homeward[bin_ids, slot]
    grad_emb = lax.dot_general(
        grad_rows, projection, (((1,), (1,)), ((), ())), preferred_element_type=jnp.float32
    ).astype(jnp.bfloat16)
    partial_w = lax.dot_general(
        embeddings, grad_rows, (((0,), (0,)), ((), ())), preferred_element_type=jnp.float32
    )
    replicas = lax.axis_size("dp")
    tokens_all = float(rows * replicas * owners)
    loss_sum = lax.psum(local_loss, ("dp", "bin"))
    weight_sum = lax.psum(partial_w, ("dp", "bin"))
    return (grad_emb, weight_sum / tokens_all, loss_sum / replicas)


def solution(mesh):
    return jax.shard_map(
        local,
        mesh=mesh,
        in_specs=(P(("dp", "bin"), None), P(("dp", "bin")), P(), P()),
        out_specs=(P(("dp", "bin"), None), P(), P()),
        check_vma=False,
    )
```

profile of v0, /device:TPU:2, one launch (start us, length us, event | category | flops | bytes accessed | tf_op | source)
XLA Modules:
  0.0 560.4 jit_solution(6354406823277336630)
XLA Ops:
  7.9 1.7 reduce-window.6
  11.6 7.6 %all-to-all-start = ((s32[32,1,1]{2,1,0:T(1,128)}), s32[32,1,1]{2,1,0:T(1,128)S(1)}, u32[]{:S(2)}, u32[]{:S(2)}) async-start(s32[32,1,1]{2,1,0:T(1,128)} %copy.13), calls=%async_computation | async-start | bytes 32768 | tf_op jit(solution)/shard_map/all_to_all | solution.py:69
  22.1 83.9 %scatter_fusion = bf16[32,48,256]{2,1,0:T(8,128)(2,1)} fusion(bf16[32,48,256]{2,1,0:T(8,128)(2,1)} %broadcast_in_dim.10, s32[768]{0:T(1024)S(1)} %get-tuple-element.160, bf16[768,256]{1,0:T(8,128)(2,1)S(1)} %convolution_convert_fusion.1), kind=kCustom, calls=%fused_computation.1 | custom fusion | bytes 1185792 | tf_op jit(solution)/shard_map/scatter | solution.py:66
  105.9 8.0 %all-to-all-start.1 = ((bf16[32,48,256]{2,1,0:T(8,128)(2,1)}), bf16[32,48,256]{2,1,0:T(8,128)(2,1)}, u32[]{:S(2)}, u32[]{:S(2)}) async-start(bf16[32,48,256]{2,1,0:T(8,128)(2,1)} %scatter_fusion), calls=%async_computation.1 | async-start | bytes 1572864 | tf_op jit(solution)/shard_map/all_to_all | solution.py:68
  115.3 2.2 collective-permute-start
  118.2 7.4 %collective-permute-done = s32[32,1]{0,1:T(1,128)S(1)} collective-permute-done((s32[32,1]{0,1:T(1,128)S(1)}, s32[32,1]{0,1:T(1,128)S(1)}, u32[]{:S(2)}, u32[]{:S(2)}) %collective-permute-start) | collective-permute-done | bytes 160 | tf_op jit(solution)/shard_map/ppermute | solution.py:10
  127.0 1.7 collective-permute-start.1
  130.3 33.9 %while.26 = (s32[]{:T(128)}, f32[]{:T(128)}, f32[3,512,256]{2,1,0:T(8,128)S(1)}, bf16[3,512,256]{2,1,0:T(8,128)(2,1)}, f32[1536]{0:T(1024)S(1)}, /*index=5*/bf16...) while((s32[]{:T(128)}, f32[]{:T(128)}, ...), condition=%wide.region_11.12_spmd.clone, body=%wide.region_7.11_spmd.clone.sunk | while | flops 822609920 | bytes 6076697 | solution.py:49
  132.3 7.0 %convert_reduce_fusion.5 = (f32[512]{0:T(512)S(1)}, bf16[512,1536]{1,0:T(8,128)(2,1)S(1)}, f32[]{:T(128)}) fusion(f32[1536]{0:T(1024)S(1)} %mul.351, f32[512]{0:T(512)S(1)} %bitcast.112, f32[]{:T(128)} %bitcast.97, f32[]{:T(128)} %bitcast.98, f32[]{:T(128)} %bitcast.99, bf16[1536,256]{1,0:T(8,128)(2,1)} %get-tuple-element.400, ...), kind=kOutput, calls=%fused_computation.11.clone.1 | convolution fusion | flops 419167744 | bytes 2641924 | tf_op jit(solution)/shard_map/while/body/eval_jaxpr/dot_general | solution.py:24
  139.2 1.8 fusion.70
  143.6 7.0 %convert_reduce_fusion.5 = (f32[512]{0:T(512)S(1)}, bf16[512,1536]{1,0:T(8,128)(2,1)S(1)}, f32[]{:T(128)}) fusion(f32[1536]{0:T(1024)S(1)} %mul.351, f32[512]{0:T(512)S(1)} %bitcast.112, f32[]{:T(128)} %bitcast.97, f32[]{:T(128)} %bitcast.98, f32[]{:T(128)} %bitcast.99, bf16[1536,256]{1,0:T(8,128)(2,1)} %get-tuple-element.400, ...), kind=kOutput, calls=%fused_computation.11.clone.1 | convolution fusion | flops 419167744 | bytes 2641924 | tf_op jit(solution)/shard_map/while/body/eval_jaxpr/dot_general | solution.py:24
  150.5 1.8 fusion.70
  154.9 7.0 %convert_reduce_fusion.5 = (f32[512]{0:T(512)S(1)}, bf16[512,1536]{1,0:T(8,128)(2,1)S(1)}, f32[]{:T(128)}) fusion(f32[1536]{0:T(1024)S(1)} %mul.351, f32[512]{0:T(512)S(1)} %bitcast.112, f32[]{:T(128)} %bitcast.97, f32[]{:T(128)} %bitcast.98, f32[]{:T(128)} %bitcast.99, bf16[1536,256]{1,0:T(8,128)(2,1)} %get-tuple-element.400, ...), kind=kOutput, calls=%fused_computation.11.clone.1 | convolution fusion | flops 419167744 | bytes 2641924 | tf_op jit(solution)/shard_map/while/body/eval_jaxpr/dot_general | solution.py:24
  161.8 1.8 fusion.70
  165.3 42.6 %while.27 = (s32[]{:T(128)}, f32[]{:T(128)}, f32[3,512,256]{2,1,0:T(8,128)S(1)}, bf16[3,512,256]{2,1,0:T(8,128)(2,1)}, f32[1536]{0:T(1024)}, /*index=5*/bf16[153...) while((s32[]{:T(128)}, f32[]{:T(128)}, ...), condition=%wide.region_18.19_spmd.clone, body=%wide.region_14.18_spmd.clone.sunk | while | flops 822609920 | bytes 9273709 | solution.py:49
  165.3 1.7 fusion.76
  170.4 6.9 %convert_reduce_fusion.6 = (f32[512]{0:T(512)S(1)}, bf16[512,1536]{1,0:T(8,128)(2,1)S(1)}, f32[]{:T(128)}) fusion(f32[1536]{0:T(1024)S(1)} %mul.354, f32[512]{0:T(512)} %bitcast.113, f32[]{:T(128)} %bitcast.108, f32[]{:T(128)} %bitcast.109, f32[]{:T(128)} %bitcast.110, bf16[1536,256]{1,0:T(8,128)(2,1)} %get-tuple-element.370, ...), kind=kOutput, calls=%fused_computation.34.clone.1 | convolution fusion | flops 419167744 | bytes 2643972 | tf_op jit(solution)/shard_map/while/body/eval_jaxpr/dot_general | solution.py:24
  184.6 6.9 %convert_reduce_fusion.6 = (f32[512]{0:T(512)S(1)}, bf16[512,1536]{1,0:T(8,128)(2,1)S(1)}, f32[]{:T(128)}) fusion(f32[1536]{0:T(1024)S(1)} %mul.354, f32[512]{0:T(512)} %bitcast.113, f32[]{:T(128)} %bitcast.108, f32[]{:T(128)} %bitcast.109, f32[]{:T(128)} %bitcast.110, bf16[1536,256]{1,0:T(8,128)(2,1)} %get-tuple-element.370, ...), kind=kOutput, calls=%fused_computation.34.clone.1 | convolution fusion | flops 419167744 | bytes 2643972 | tf_op jit(solution)/shard_map/while/body/eval_jaxpr/dot_general | solution.py:24
  193.7 1.7 fusion.76
  198.8 6.9 %convert_reduce_fusion.6 = (f32[512]{0:T(512)S(1)}, bf16[512,1536]{1,0:T(8,128)(2,1)S(1)}, f32[]{:T(128)}) fusion(f32[1536]{0:T(1024)S(1)} %mul.354, f32[512]{0:T(512)} %bitcast.113, f32[]{:T(128)} %bitcast.108, f32[]{:T(128)} %bitcast.109, f32[]{:T(128)} %bitcast.110, bf16[1536,256]{1,0:T(8,128)(2,1)} %get-tuple-element.370, ...), kind=kOutput, calls=%fused_computation.34.clone.1 | convolution fusion | flops 419167744 | bytes 2643972 | tf_op jit(solution)/shard_map/while/body/eval_jaxpr/dot_general | solution.py:24
  209.1 7.4 %all-to-all-start.2 = ((bf16[32,48,256]{2,1,0:T(8,128)(2,1)}), bf16[32,48,256]{2,1,0:T(8,128)(2,1)S(1)}, u32[]{:S(2)}, u32[]{:S(2)}) async-start(bf16[32,48,256]{2,1,0:T(8,128)(2,1)} %bitcast.111), calls=%async_computation.2 | async-start | bytes 1572864 | tf_op jit(solution)/shard_map/all_to_all | solution.py:87
  216.6 80.5 %psum.15 = f32[]{:T(128)} all-reduce(f32[]{:T(128)S(6)} %add.95), channel_id=1, replica_groups=mesh['dp'=8,'bin'=32] {'dp','bin'}, use_global_device_ids=true, to_apply=%region_20.21 | all-reduce | flops 1 | bytes 8 | tf_op jit(solution)/shard_map/psum | solution.py:99
  297.8 4.4 gather_fusion
  304.4 246.2 %all-reduce.2.cloned.1.call-done = f32[256,256]{0,1:T(8,128)} async-done(((f32[256,256]{0,1:T(8,128)}), f32[256,256]{0,1:T(8,128)}) %all-reduce.2.cloned.1.call-update) | async-done | bytes 262160 | tf_op jit(solution)/shard_map/psum | solution.py:100
  (89 shorter events, 37.4 us)
Async XLA Ops:
  7.2 12.8 %copy-start = (bf16[768,256]{1,0:T(8,128)(2,1)S(1)}, bf16[768,256]{1,0:T(8,128)(2,1)}, u32[]{:S(2)}) copy-start(bf16[768,256]{1,0:T(8,128)(2,1)} %param.8) | copy-start | bytes 1179652
  11.6 94.4 %all-to-all-start = ((s32[32,1,1]{2,1,0:T(1,128)}), s32[32,1,1]{2,1,0:T(1,128)S(1)}, u32[]{:S(2)}, u32[]{:S(2)}) async-start(s32[32,1,1]{2,1,0:T(1,128)} %copy.13), calls=%async_computation | async-start | bytes 32768 | tf_op jit(solution)/shard_map/all_to_all | solution.py:69
  105.9 8.0 %copy-start.7 = (f32[3]{0:T(128)S(1)}, f32[3]{0:T(128)}, u32[]{:S(2)}) copy-start(f32[3]{0:T(128)} %param.10) | copy-start | bytes 40
  105.9 21.0 %all-to-all-start.1 = ((bf16[32,48,256]{2,1,0:T(8,128)(2,1)}), bf16[32,48,256]{2,1,0:T(8,128)(2,1)}, u32[]{:S(2)}, u32[]{:S(2)}) async-start(bf16[32,48,256]{2,1,0:T(8,128)(2,1)} %scatter_fusion), calls=%async_computation.1 | async-start | bytes 1572864 | tf_op jit(solution)/shard_map/all_to_all | solution.py:68
  115.3 10.3 %collective-permute-start = (s32[32,1]{0,1:T(1,128)S(1)}, s32[32,1]{0,1:T(1,128)S(1)}, u32[]{:S(2)}, u32[]{:S(2)}) collective-permute-start(s32[32,1]{0,1:T(1,128)S(1)} %bitcast.115), channel_id=1, source_target_pairs={{0,16},{1,17},{2,18},{3,19},{4,20},{5,21},{6,22},{7,23},{8,24},{9,... | collective-permute-start | bytes 392 | tf_op jit(solution)/shard_map/ppermute | solution.py:10
  125.6 4.7 copy-start.6
  127.0 37.3 %collective-permute-start.1 = (bf16[1536,256]{1,0:T(8,128)(2,1)}, bf16[1536,256]{1,0:T(8,128)(2,1)S(1)}, u32[]{:S(2)}, u32[]{:S(2)}) collective-permute-start(bf16[1536,256]{1,0:T(8,128)(2,1)} %bitcast.4), channel_id=1, source_target_pairs={{0,16},{1,17},{2,18},{3,19},{4,20},{5,21},{6,22},{7,23},{8,24},{9,... | collective-permute-start | bytes 2359304 | tf_op jit(solution)/shard_map/ppermute | solution.py:10
  164.3 0.9 copy-start.1
  165.3 2.9 copy-start.4
  170.4 6.9 %copy-start.2 = (bf16[1536,256]{1,0:T(8,128)(2,1)S(1)}, bf16[1536,256]{1,0:T(8,128)(2,1)}, u32[]{:S(2)}) copy-start(bf16[1536,256]{1,0:T(8,128)(2,1)} %get-tuple-element.370) | copy-start | bytes 2359300 | tf_op jit(solution)/shard_map/while
  177.3 2.2 copy-start.5
  179.5 2.9 copy-start.4
  184.6 7.0 %copy-start.2 = (bf16[1536,256]{1,0:T(8,128)(2,1)S(1)}, bf16[1536,256]{1,0:T(8,128)(2,1)}, u32[]{:S(2)}) copy-start(bf16[1536,256]{1,0:T(8,128)(2,1)} %get-tuple-element.370) | copy-start | bytes 2359300 | tf_op jit(solution)/shard_map/while
  191.5 2.2 copy-start.5
  193.7 2.9 copy-start.4
  198.8 7.0 %copy-start.2 = (bf16[1536,256]{1,0:T(8,128)(2,1)S(1)}, bf16[1536,256]{1,0:T(8,128)(2,1)}, u32[]{:S(2)}) copy-start(bf16[1536,256]{1,0:T(8,128)(2,1)} %get-tuple-element.370) | copy-start | bytes 2359300 | tf_op jit(solution)/shard_map/while
  205.7 2.2 copy-start.5
  209.1 88.7 %all-to-all-start.2 = ((bf16[32,48,256]{2,1,0:T(8,128)(2,1)}), bf16[32,48,256]{2,1,0:T(8,128)(2,1)S(1)}, u32[]{:S(2)}, u32[]{:S(2)}) async-start(bf16[32,48,256]{2,1,0:T(8,128)(2,1)} %bitcast.111), calls=%async_computation.2 | async-start | bytes 1572864 | tf_op jit(solution)/shard_map/all_to_all | solution.py:87
  216.5 334.1 %all-reduce.2.cloned.1.call-start = ((), (), s32[]{:S(2)}) async-start(), calls=%async_computation.3 | async-start | bytes 524288 | tf_op jit(solution)/shard_map/psum | solution.py:100
  297.8 5.5 copy-start.3
Sparse Core Ops, SparseCore 0:
  303.4 247.0 all-reduce.1
where the time goes:
time: 564 us; the launch traced here: 560 us
  waiting for transfers between devices  254 us (45%)
  local copies, waits for them, and re-layouts  99.8 us (18%)
  blocking collectives  80.5 us (14%)
  matrix products  54.8 us (10%)
  starting transfers between devices  26.9 us (5%)
  other arithmetic  23.1 us (4%)
  between operations  17.5 us (3%)
    psum x1, waiting for transfers between devices, local(): weight_sum = lax.psum(partial_w, ('dp', 'bin'))  246 us
    scatter x1, local copies, waits for them, and re-layouts, local(): jnp.zeros((owners, slots_per, width), jnp.bfloat16).at[bin_ids, slot]  83.9 us
    psum x1, blocking collectives, local(): loss_sum = lax.psum(local_loss, ('dp', 'bin'))  80.5 us
    dot_general x6, matrix products, step(): lax.dot_general(xblk, xb, (((1,), (1,)), ((), ())), preferred_element_typ...  41.7 us
  transfers between devices with their start and end apart: 6, of which 2 were waited for; matrix products, arithmetic and copies ran while one was open for 22% of the time, Pallas kernels for 0%

commit v1 on v0

--- a/solution.py
+++ b/solution.py
@@ -97,7 +97,7 @@
     replicas = lax.axis_size("dp")
     tokens_all = float(rows * replicas * owners)
     loss_sum = lax.psum(local_loss, ("dp", "bin"))
-    weight_sum = lax.psum(partial_w, ("dp", "bin"))
+    weight_sum = lax.psum(lax.psum(partial_w, "bin"), "dp")
     return (grad_emb, weight_sum / tokens_all, loss_sum / replicas)
 
 

time: 564 us -> 446 us (0.79)
  waiting for transfers between devices: 254 us -> 120 us
  blocking collectives: 80.5 us -> 95.2 us
  matrix products: 54.8 us -> 64.3 us
  starting transfers between devices: 26.9 us -> 19 us
    psum x1 -> x2, waiting for transfers between devices: 246 us -> 112 us  [local(): weight_sum = lax.psum(lax.psum(partial_w, 'bin'), 'dp')]
    all_to_all x0 -> x1, blocking collectives: none -> 19.2 us  [local(): lax.all_to_all(grad_feat.reshape(owners, slots_per, width), 'bin', split_...]
    all_to_all x1 -> x0, starting transfers between devices: 7.39 us -> none  [local(): lax.all_to_all(grad_feat.reshape(owners, slots_per, width), 'bin', split_...]
    dot_general x6, matrix products: 41.7 us -> 47.6 us  [step(): lax.dot_general(xblk, xb, (((1,), (1,)), ((), ())), preferred_element_typ...]
  transfers between devices with their start and end apart: 6 -> 6, of which waited for: 2 -> 2; matrix products, arithmetic and copies ran while one was open for 22% -> 29% of each run, Pallas kernels for 0% -> 0%
where the time goes in v1:
time: 446 us; the launch traced here: 440 us
  waiting for transfers between devices  120 us (27%)
  local copies, waits for them, and re-layouts  102 us (23%)
  blocking collectives  95.2 us (21%)
  matrix products  64.3 us (14%)
  starting transfers between devices  19 us (4%)
  other arithmetic  18.5 us (4%)
  between operations  17.5 us (4%)
    psum x2, waiting for transfers between devices, local(): weight_sum = lax.psum(lax.psum(partial_w, 'bin'), 'dp')  112 us
    scatter x1, local copies, waits for them, and re-layouts, local(): jnp.zeros((owners, slots_per, width), jnp.bfloat16).at[bin_ids, slot]  84.2 us
    psum x1, blocking collectives, local(): loss_sum = lax.psum(local_loss, ('dp', 'bin'))  76 us
    dot_general x6, matrix products, step(): lax.dot_general(xblk, xb, (((1,), (1,)), ((), ())), preferred_element_typ...  47.6 us
    all_to_all x1, blocking collectives, local(): lax.all_to_all(grad_feat.reshape(owners, slots_per, width), 'bin', split_...  19.2 us
    dot_general x6, matrix products, step(): jnp.dot(gram, xb, preferred_element_type=jnp.float32)  13.5 us
  transfers between devices with their start and end apart: 6, of which 2 were waited for; matrix products, arithmetic and copies ran while one was open for 29% of the time, Pallas kernels for 0%

profile of v1, /device:TPU:2, one launch (start us, length us, event | category | flops | bytes accessed | tf_op | source)
XLA Modules:
  0.0 440.1 jit_solution(4670000145724406830)
XLA Ops:
  7.9 1.7 reduce-window.6
  11.6 7.6 %all-to-all-start = ((s32[32,1,1]{2,1,0:T(1,128)}), s32[32,1,1]{2,1,0:T(1,128)S(1)}, u32[]{:S(2)}, u32[]{:S(2)}) async-start(s32[32,1,1]{2,1,0:T(1,128)} %copy.13), calls=%async_computation | async-start | bytes 32768 | tf_op jit(solution)/shard_map/all_to_all | solution.py:69
  22.0 84.2 %scatter_fusion = bf16[32,48,256]{2,1,0:T(8,128)(2,1)} fusion(bf16[32,48,256]{2,1,0:T(8,128)(2,1)} %broadcast_in_dim.10, s32[768]{0:T(1024)S(1)} %get-tuple-element.160, bf16[768,256]{1,0:T(8,128)(2,1)S(1)} %convolution_convert_fusion.1), kind=kCustom, calls=%fused_computation.1 | custom fusion | bytes 1185792 | tf_op jit(solution)/shard_map/scatter | solution.py:66
  106.3 7.4 %all-to-all-start.1 = ((bf16[32,48,256]{2,1,0:T(8,128)(2,1)}), bf16[32,48,256]{2,1,0:T(8,128)(2,1)}, u32[]{:S(2)}, u32[]{:S(2)}) async-start(bf16[32,48,256]{2,1,0:T(8,128)(2,1)} %scatter_fusion), calls=%async_computation.1 | async-start | bytes 1572864 | tf_op jit(solution)/shard_map/all_to_all | solution.py:68
  115.1 2.2 collective-permute-start
  118.0 7.4 %collective-permute-done = s32[32,1]{0,1:T(1,128)S(1)} collective-permute-done((s32[32,1]{0,1:T(1,128)S(1)}, s32[32,1]{0,1:T(1,128)S(1)}, u32[]{:S(2)}, u32[]{:S(2)}) %collective-permute-start) | collective-permute-done | bytes 160 | tf_op jit(solution)/shard_map/ppermute | solution.py:10
  130.1 38.2 %while.26 = (s32[]{:T(128)}, f32[]{:T(128)}, f32[3,512,256]{2,1,0:T(8,128)S(1)}, bf16[3,512,256]{2,1,0:T(8,128)(2,1)}, f32[1536]{0:T(1024)S(1)}, /*index=5*/bf16...) while((s32[]{:T(128)}, f32[]{:T(128)}, ...), condition=%wide.region_11.12_spmd.clone, body=%wide.region_7.11_spmd.clone.sunk | while | flops 822609920 | bytes 6076197 | solution.py:49
  132.0 8.0 %convert_reduce_fusion.5 = (f32[512]{0:T(512)S(1)}, bf16[512,1536]{1,0:T(8,128)(2,1)}, f32[]{:T(128)}) fusion(f32[1536]{0:T(1024)S(1)} %mul.351, f32[512]{0:T(512)S(1)} %bitcast.112, f32[]{:T(128)} %bitcast.97, f32[]{:T(128)} %bitcast.98, f32[]{:T(128)} %bitcast.99, bf16[1536,256]{1,0:T(8,128)(2,1)} %get-tuple-element.400, ...), kind=kOutput, calls=%fused_computation.11.clone.1 | convolution fusion | flops 419167744 | bytes 2641416 | tf_op jit(solution)/shard_map/while/body/eval_jaxpr/dot_general | solution.py:24
  140.6 2.2 fusion.70
  144.7 8.0 %convert_reduce_fusion.5 = (f32[512]{0:T(512)S(1)}, bf16[512,1536]{1,0:T(8,128)(2,1)}, f32[]{:T(128)}) fusion(f32[1536]{0:T(1024)S(1)} %mul.351, f32[512]{0:T(512)S(1)} %bitcast.112, f32[]{:T(128)} %bitcast.97, f32[]{:T(128)} %bitcast.98, f32[]{:T(128)} %bitcast.99, bf16[1536,256]{1,0:T(8,128)(2,1)} %get-tuple-element.400, ...), kind=kOutput, calls=%fused_computation.11.clone.1 | convolution fusion | flops 419167744 | bytes 2641416 | tf_op jit(solution)/shard_map/while/body/eval_jaxpr/dot_general | solution.py:24
  153.3 2.2 fusion.70
  157.5 8.0 %convert_reduce_fusion.5 = (f32[512]{0:T(512)S(1)}, bf16[512,1536]{1,0:T(8,128)(2,1)}, f32[]{:T(128)}) fusion(f32[1536]{0:T(1024)S(1)} %mul.351, f32[512]{0:T(512)S(1)} %bitcast.112, f32[]{:T(128)} %bitcast.97, f32[]{:T(128)} %bitcast.98, f32[]{:T(128)} %bitcast.99, bf16[1536,256]{1,0:T(8,128)(2,1)} %get-tuple-element.400, ...), kind=kOutput, calls=%fused_computation.11.clone.1 | convolution fusion | flops 419167744 | bytes 2641416 | tf_op jit(solution)/shard_map/while/body/eval_jaxpr/dot_general | solution.py:24
  166.0 2.2 fusion.70
  169.3 45.8 %while.27 = (s32[]{:T(128)}, f32[]{:T(128)}, f32[3,512,256]{2,1,0:T(8,128)S(1)}, bf16[3,512,256]{2,1,0:T(8,128)(2,1)}, f32[1536]{0:T(1024)}, /*index=5*/bf16[153...) while((s32[]{:T(128)}, f32[]{:T(128)}, ...), condition=%wide.region_18.19_spmd.clone, body=%wide.region_14.18_spmd.clone.sunk | while | flops 822609920 | bytes 6079325 | solution.py:49
  173.9 7.9 %convert_reduce_fusion.6 = (f32[512]{0:T(512)}, bf16[512,1536]{1,0:T(8,128)(2,1)}, f32[]{:T(128)}) fusion(f32[1536]{0:T(1024)S(1)} %mul.354, f32[512]{0:T(512)S(1)} %bitcast.113, f32[]{:T(128)} %bitcast.108, f32[]{:T(128)} %bitcast.109, f32[]{:T(128)} %bitcast.110, bf16[1536,256]{1,0:T(8,128)(2,1)} %get-tuple-element.370, ...), kind=kOutput, calls=%fused_computation.34.clone.1 | convolution fusion | flops 419167744 | bytes 2643464 | tf_op jit(solution)/shard_map/while/body/eval_jaxpr/dot_general | solution.py:24
  182.3 2.3 fusion.77
  189.1 7.9 %convert_reduce_fusion.6 = (f32[512]{0:T(512)}, bf16[512,1536]{1,0:T(8,128)(2,1)}, f32[]{:T(128)}) fusion(f32[1536]{0:T(1024)S(1)} %mul.354, f32[512]{0:T(512)S(1)} %bitcast.113, f32[]{:T(128)} %bitcast.108, f32[]{:T(128)} %bitcast.109, f32[]{:T(128)} %bitcast.110, bf16[1536,256]{1,0:T(8,128)(2,1)} %get-tuple-element.370, ...), kind=kOutput, calls=%fused_computation.34.clone.1 | convolution fusion | flops 419167744 | bytes 2643464 | tf_op jit(solution)/shard_map/while/body/eval_jaxpr/dot_general | solution.py:24
  197.6 2.3 fusion.77
  204.4 7.9 %convert_reduce_fusion.6 = (f32[512]{0:T(512)}, bf16[512,1536]{1,0:T(8,128)(2,1)}, f32[]{:T(128)}) fusion(f32[1536]{0:T(1024)S(1)} %mul.354, f32[512]{0:T(512)S(1)} %bitcast.113, f32[]{:T(128)} %bitcast.108, f32[]{:T(128)} %bitcast.109, f32[]{:T(128)} %bitcast.110, bf16[1536,256]{1,0:T(8,128)(2,1)} %get-tuple-element.370, ...), kind=kOutput, calls=%fused_computation.34.clone.1 | convolution fusion | flops 419167744 | bytes 2643464 | tf_op jit(solution)/shard_map/while/body/eval_jaxpr/dot_general | solution.py:24
  212.9 2.3 fusion.77
  215.5 19.2 %all_to_all.22 = bf16[32,48,256]{2,1,0:T(8,128)(2,1)S(1)} all-to-all(bf16[32,48,256]{2,1,0:T(8,128)(2,1)S(1)} %bitcast.111), channel_id=1, replica_groups=mesh['dp'=8,'bin'=32] {'bin'}, dimensions={0} | all-to-all | bytes 1572864 | tf_op jit(solution)/shard_map/all_to_all | solution.py:87
  234.7 4.4 %gather_fusion = bf16[768,256]{1,0:T(8,128)(2,1)S(1)} fusion(bf16[32,48,256]{2,1,0:T(8,128)(2,1)S(1)} %all_to_all.22, s32[768]{0:T(1024)S(1)} %get-tuple-element.159), kind=kCustom, calls=%fused_computation | custom fusion | bytes 792576 | tf_op jit(solution)/shard_map/gather | solution.py:90
  240.2 112.4 %all-reduce.3.cloned.1.call-done = f32[256,256]{0,1:T(8,128)} async-done(((f32[256,256]{0,1:T(8,128)}), f32[256,256]{0,1:T(8,128)}) %all-reduce.3.cloned.1.call-update) | async-done | bytes 262160 | tf_op jit(solution)/shard_map/psum | solution.py:100
  352.7 76.0 %psum.23 = f32[]{:T(128)} all-reduce(f32[]{:T(128)S(6)} %add.97), channel_id=1, replica_groups=mesh['dp'=8,'bin'=32] {'dp','bin'}, use_global_device_ids=true, to_apply=%region_21.22 | all-reduce | flops 1 | bytes 8 | tf_op jit(solution)/shard_map/psum | solution.py:99
  (85 shorter events, 35.3 us)
Async XLA Ops:
  7.2 12.8 %copy-start = (bf16[768,256]{1,0:T(8,128)(2,1)S(1)}, bf16[768,256]{1,0:T(8,128)(2,1)}, u32[]{:S(2)}) copy-start(bf16[768,256]{1,0:T(8,128)(2,1)} %param.8) | copy-start | bytes 1179652
  11.6 94.7 %all-to-all-start = ((s32[32,1,1]{2,1,0:T(1,128)}), s32[32,1,1]{2,1,0:T(1,128)S(1)}, u32[]{:S(2)}, u32[]{:S(2)}) async-start(s32[32,1,1]{2,1,0:T(1,128)} %copy.13), calls=%async_computation | async-start | bytes 32768 | tf_op jit(solution)/shard_map/all_to_all | solution.py:69
  106.3 7.5 %copy-start.6 = (f32[3]{0:T(128)S(1)}, f32[3]{0:T(128)}, u32[]{:S(2)}) copy-start(f32[3]{0:T(128)} %param.10) | copy-start | bytes 40
  106.3 20.4 %all-to-all-start.1 = ((bf16[32,48,256]{2,1,0:T(8,128)(2,1)}), bf16[32,48,256]{2,1,0:T(8,128)(2,1)}, u32[]{:S(2)}, u32[]{:S(2)}) async-start(bf16[32,48,256]{2,1,0:T(8,128)(2,1)} %scatter_fusion), calls=%async_computation.1 | async-start | bytes 1572864 | tf_op jit(solution)/shard_map/all_to_all | solution.py:68
  113.7 238.9 %all-reduce.3.cloned.1.call-start = ((), (), s32[]{:S(2)}) async-start(), calls=%async_computation.3 | async-start | bytes 524288 | tf_op jit(solution)/shard_map/psum | solution.py:100
  115.1 10.3 %collective-permute-start = (s32[32,1]{0,1:T(1,128)S(1)}, s32[32,1]{0,1:T(1,128)S(1)}, u32[]{:S(2)}, u32[]{:S(2)}) collective-permute-start(s32[32,1]{0,1:T(1,128)S(1)} %bitcast.115), channel_id=1, source_target_pairs={{0,16},{1,17},{2,18},{3,19},{4,20},{5,21},{6,22},{7,23},{8,24},{9,... | collective-permute-start | bytes 392 | tf_op jit(solution)/shard_map/ppermute | solution.py:10
  126.7 41.6 %collective-permute-start.1 = (bf16[1536,256]{1,0:T(8,128)(2,1)}, bf16[1536,256]{1,0:T(8,128)(2,1)S(1)}, u32[]{:S(2)}, u32[]{:S(2)}) collective-permute-start(bf16[1536,256]{1,0:T(8,128)(2,1)} %bitcast.4), channel_id=1, source_target_pairs={{0,16},{1,17},{2,18},{3,19},{4,20},{5,21},{6,22},{7,23},{8,24},{9,... | collective-permute-start | bytes 2359304 | tf_op jit(solution)/shard_map/ppermute | solution.py:10
  168.3 0.9 copy-start.3
  168.3 0.9 copy-start.1
  169.3 0.6 copy-start.4
  182.3 2.3 copy-start.5
  184.6 0.6 copy-start.4
  197.6 2.3 copy-start.5
  199.9 0.6 copy-start.4
  212.9 2.3 copy-start.5
  239.1 190.2 %copy-start.2 = (bf16[256,256]{1,0:T(8,128)(2,1)S(1)}, bf16[256,256]{1,0:T(8,128)(2,1)}, u32[]{:S(2)}) copy-start(bf16[256,256]{1,0:T(8,128)(2,1)} %param.11) | copy-start | bytes 393220
  240.1 190.2 %all-reduce.5.cloned.1.call-start = ((), (), s32[]{:S(2)}) async-start(), calls=%async_computation.4 | async-start | bytes 524288 | tf_op jit(solution)/shard_map/psum | solution.py:100
Sparse Core Ops, SparseCore 0:
  240.2 112.2 all-reduce.2
  355.0 72.7 all-reduce.4
